TPU v7x, 32 devices: a whole 2x2x4 slice. The times are simulated.
32 devices in a mesh: vocab: 4 (over z), rows: 8 (over y, x, core).
Axes of the slice: x: 2, y: 2, z: 4, core: 2. Of those that a mesh axis runs over, the one named last changes fastest.
Arguments:
- hidden_pass: bfloat16 [96, 64, 4096], P('rows', None, 'vocab'), may hold values from -6 to 6
- hidden_query: bfloat16 [96, 8, 4096], P('rows', None, 'vocab'), may hold values from -6 to 6
- mask_pass: int32 [96, 64], P('rows'), may hold values 0 or 1
- mask_query: int32 [96, 8], P('rows'), may hold values 0 or 1
- labels: int32 [96], P('rows'), may hold values from 0 to 95, each once
- head_weight: bfloat16 [4096, 16384], P('rows', 'vocab'), may hold values from -1 to 1
Outputs:
- grad_pass: bfloat16 [96, 64, 4096], P('rows', None, 'vocab')
- grad_query: bfloat16 [96, 8, 4096], P('rows', None, 'vocab')
Inputs may be any that keep to these rules, and one draw needn't show every extreme that they name: `labels`: each passage is the positive of exactly one query.
All inputs are finite; a program needn't handle non-finite values. No bound on the sum of `mask_pass` or of `mask_query` on one device may be relied on, other than what follows from the above.
Results may differ from a plain program's by a relative error of at most 0.018.
The roundings to bfloat16 on the way count: a program that leaves them out, or rounds other values in their place, can miss the bound.
Values may be sent and summed in bfloat16 or wider, within the bound.
No kernel may reach another device: no remote copies, remote signals or barrier semaphores. Data moves between devices by JAX's collectives and lax.ppermute only.
A program may use at most 128 MiB of HBM per device.

v0:
```python
import jax
import jax.numpy as jnp
from jax import lax
from jax.sharding import PartitionSpec as P

V = 16384
MARGIN = 1.0
SHARPNESS = 16.0


def activate(logits):
    return jnp.log1p(jnp.maximum(logits, 0.0))


def pool_rows(logits, mask, groups, length):
    values = activate(logits).reshape(groups, length, -1)
    weight = mask.astype(jnp.float32)[:, :, None]
    totals = jnp.sum(values**4 * weight, axis=1)
    sparse = (jnp.power(totals + 1.0, 0.25) - 1.0).astype(jnp.bfloat16)
    return (values, totals, sparse)


def logit_slopes(sparse_grad, values, totals, logits, mask, groups, length):
    weight = mask.astype(jnp.float32)[:, :, None]
    factor = sparse_grad * jnp.power(totals + 1.0, -0.75)
    slopes = 1.0 / (1.0 + jnp.maximum(logits, 0.0)).reshape(groups, length, -1)
    gradient = factor[:, None, :] * weight * values**3 * slopes
    return gradient.astype(jnp.bfloat16).reshape(groups * length, -1)


def shards(hidden_pass, hidden_query, mask_pass, mask_query, labels, head_weight):
    groups = hidden_pass.shape[0]
    pass_length = hidden_pass.shape[1]
    query_length = hidden_query.shape[1]
    pass_rows = groups * pass_length
    whole_pass, whole_query = (
        lax.all_gather(hidden_pass, "vocab", axis=2, tiled=True),
        lax.all_gather(hidden_query, "vocab", axis=2, tiled=True),
    )
    tokens = jnp.concatenate(
        [whole_pass.reshape(pass_rows, -1), whole_query.reshape(groups * query_length, -1)], axis=0
    )
    whole_head = lax.all_gather(head_weight, "rows", axis=0, tiled=True)
    logits = jnp.dot(tokens, whole_head, preferred_element_type=jnp.float32)
    logits_pass = logits[:pass_rows]
    logits_query = logits[pass_rows:]
    values_pass, totals_pass, sparse_pass = pool_rows(logits_pass, mask_pass, groups, pass_length)
    values_query, totals_query, sparse_query = pool_rows(
        logits_query, mask_query, groups, query_length
    )
    all_pass = lax.all_gather(sparse_pass, "rows", axis=0, tiled=True)
    partial_scores = lax.dot_general(
        sparse_query, all_pass, (((1,), (1,)), ((), ())), preferred_element_type=jnp.float32
    )
    scaling = SHARPNESS * V ** (-0.5)
    scores = lax.psum(partial_scores, "vocab") * scaling
    onehot = (labels[:, None] == jnp.arange(all_pass.shape[0], dtype=jnp.int32)[None, :]).astype(
        jnp.float32
    )
    positive = jnp.sum(scores * onehot, axis=1, keepdims=True)
    weights = jax.nn.sigmoid(MARGIN + scores - positive) * (1.0 - onehot)
    score_grad = ((weights - onehot * jnp.sum(weights, axis=1, keepdims=True)) * scaling).astype(
        jnp.bfloat16
    )
    query_sparse_grad = jnp.dot(score_grad, all_pass, preferred_element_type=jnp.float32)
    pass_sparse_grad = lax.psum_scatter(
        lax.dot_general(
            score_grad, sparse_query, (((0,), (0,)), ((), ())), preferred_element_type=jnp.float32
        ).astype(jnp.bfloat16),
        "rows",
        scatter_dimension=0,
        tiled=True,
    ).astype(jnp.float32)
    slopes_pass = logit_slopes(
        pass_sparse_grad, values_pass, totals_pass, logits_pass, mask_pass, groups, pass_length
    )
    slopes_query = logit_slopes(
        query_sparse_grad,
        values_query,
        totals_query,
        logits_query,
        mask_query,
        groups,
        query_length,
    )
    slopes = jnp.concatenate([slopes_pass, slopes_query], axis=0)
    partial_terms = lax.dot_general(
        slopes, whole_head, (((1,), (1,)), ((), ())), preferred_element_type=jnp.float32
    )
    summed = lax.psum_scatter(
        partial_terms.astype(jnp.bfloat16), "vocab", scatter_dimension=1, tiled=True
    ).astype(jnp.float32)
    grad_pass = summed[:pass_rows].reshape(groups, pass_length, -1).astype(jnp.bfloat16)
    grad_query = summed[pass_rows:].reshape(groups, query_length, -1).astype(jnp.bfloat16)
    return (grad_pass, grad_query)


def solution(mesh):
    return jax.shard_map(
        shards,
        mesh=mesh,
        in_specs=(
            P("rows", None, "vocab"),
            P("rows", None, "vocab"),
            P("rows", None),
            P("rows", None),
            P("rows"),
            P("rows", "vocab"),
        ),
        out_specs=(P("rows", None, "vocab"), P("rows", None, "vocab")),
        check_vma=False,
    )
```

profile of v0, /device:TPU:0, one launch (start us, length us, event | category | flops | bytes accessed | tf_op | source)
XLA Modules:
  0.0 589.9 jit_solution(8366883273311622980)
XLA Ops:
  7.2 0.7 all-gather.4.cloned.1.call-update
  7.9 0.7 all-gather.6.cloned.1.call-update
  8.7 0.7 convert_element_type.48
  9.4 0.7 convert_element_type.46
  10.3 1.2 dynamic-slice.4
  12.2 29.5 %all_gather.13 = bf16[12,8,4096]{2,1,0:T(8,128)(2,1)S(1)} all-gather(bf16[12,8,1024]{2,1,0:T(8,128)(2,1)} %param.7), channel_id=1, replica_groups=mesh['vocab'=4,'rows'=8] {'vocab'}, dimensions={2}, use_global_device_ids=true | all-gather | bytes 983040 | tf_op jit(solution)/shard_map/all_gather | solution.py:38
  41.7 91.9 %all-gather.4.cloned.1.call-done = bf16[12,64,4096]{2,1,0:T(8,128)(2,1)} async-done(((bf16[12,64,1024]{2,1,0:T(8,128)(2,1)}), bf16[12,64,4096]{2,1,0:T(8,128)(2,1)}) %all-gather.4.cloned.1.call-update) | async-done | bytes 6291472 | tf_op jit(solution)/shard_map/all_gather | solution.py:37
  133.5 162.8 %all-gather.6.cloned.1.call-done = bf16[4096,4096]{1,0:T(8,128)(2,1)} async-done(((bf16[512,4096]{1,0:T(8,128)(2,1)}), bf16[4096,4096]{1,0:T(8,128)(2,1)}) %all-gather.6.cloned.1.call-update) | async-done | bytes 33554448 | tf_op jit(solution)/shard_map/all_gather | solution.py:43
  296.3 36.8 %fusion.4 = f32[864,4096]{1,0:T(8,128)} fusion(bf16[4096,4096]{1,0:T(8,128)(2,1)} %all-gather.6.cloned.1.call-done, bf16[96,4096]{1,0:T(8,128)(2,1)S(1)} %bitcast.31, bf16[768,4096]{1,0:T(8,128)(2,1)} %bitcast.32), kind=kOutput, calls=%fused_computation.8 | convolution fusion | flops 29005185024 | bytes 54788096 | tf_op jit(solution)/shard_map/dot_general | solution.py:44
  333.1 14.0 %multiply_multiply_fusion.1 = f32[768,4096]{1,0:T(8,128)} fusion(f32[864,4096]{1,0:T(8,128)} %fusion.4), kind=kLoop, calls=%fused_computation.1 | loop fusion | flops 9437184 | bytes 25165824 | tf_op jit(solution)/shard_map/mul | solution.py:18
  347.1 2.4 fusion.17
  349.6 6.6 %multiply_reduce_fusion = f32[12,4096]{1,0:T(8,128)S(1)} fusion(f32[12,64,4096]{2,1,0:T(8,128)} %bitcast.29, f32[12,64]{1,0:T(8,128)S(1)} %convert_element_type.48), kind=kLoop, calls=%fused_computation.7 | loop fusion | flops 6242304 | bytes 12782592 | tf_op jit(solution)/shard_map/reduce_sum | solution.py:18
  356.3 10.9 %all-gather = bf16[8,12,4096]{2,1,0:T(8,128)(2,1)S(1)} all-gather(bf16[1,12,4096]{2,1,0:T(8,128)(2,1)S(1)} %fusion.21), channel_id=1, replica_groups=mesh['vocab'=4,'rows'=8] {'rows'}, dimensions={0}, use_global_device_ids=true | all-gather | bytes 884736 | tf_op jit(solution)/shard_map/all_gather | solution.py:51
  367.2 0.2 reshape.38
  367.4 0.3 fusion.22
  367.7 11.8 %psum.7 = f32[12,96]{1,0:T(8,128)S(1)} all-reduce(f32[12,96]{1,0:T(8,128)S(1)} %fusion.22), channel_id=1, replica_groups=mesh['vocab'=4,'rows'=8] {'vocab'}, use_global_device_ids=true, to_apply=%region_2.0 | all-reduce | flops 1152 | bytes 9216 | tf_op jit(solution)/shard_map/psum | solution.py:56
  379.5 0.2 select_reduce_fusion
  379.7 0.2 fusion.31
  379.9 0.5 convolution_convert_fusion
  380.4 18.0 %fusion = bf16[16,4096]{1,0:T(8,128)(2,1)S(1)} fusion(bf16[96,4096]{1,0:T(8,128)(2,1)S(1)} %convolution_convert_fusion), kind=kCustom, calls=%all-reduce-scatter | all-reduce-scatter fusion | flops 524289 | bytes 918016
  398.5 1.3 collective-permute-start
  399.8 0.3 convolution_multiply_fusion
  400.1 3.0 collective-permute-start.1
  403.1 2.3 fusion.20
  405.4 0.2 collective-permute-done.1
  405.6 0.8 concatenate.8
  406.5 0.2 power_multiply_fusion
  406.6 11.0 %fusion.3 = bf16[768,4096]{1,0:T(8,128)(2,1)} fusion(f32[864,4096]{1,0:T(8,128)} %fusion.4, f32[768]{0:T(1024)S(1)} %mul.135, f32[12,4096]{1,0:T(8,128)S(1)} %power_multiply_fusion), kind=kLoop, calls=%fused_computation.4 | loop fusion | flops 28311552 | bytes 19074048 | tf_op jit(solution)/shard_map/convert_element_type | solution.py:28
  417.7 36.4 %fusion.12 = bf16[864,4096]{1,0:T(8,128)(2,1)} fusion(bf16[4096,4096]{1,0:T(8,128)(2,1)} %all-gather.6.cloned.1.call-done, bf16[96,4096]{1,0:T(8,128)(2,1)S(1)} %fusion.20, bf16[768,4096]{1,0:T(8,128)(2,1)} %fusion.3), kind=kOutput, calls=%fused_computation.16 | convolution fusion | flops 29008723968 | bytes 47710208 | tf_op jit(solution)/shard_map/dot_general | solution.py:87
  454.1 125.0 %reduce-scatter.4.cloned.1.call-done = bf16[864,1024]{1,0:T(8,128)(2,1)} async-done(((bf16[864,4096]{1,0:T(8,128)(2,1)}), bf16[864,1024]{1,0:T(8,128)(2,1)}) %reduce-scatter.4.cloned.1.call-update) | async-done | bytes 1769488 | tf_op jit(solution)/shard_map/reduce_scatter | solution.py:90
  579.1 2.7 slice.20
  581.7 1.6 slice_bitcast_fusion
  (12 shorter events, 0.5 us)
Async XLA Ops:
  7.2 126.4 %all-gather.4.cloned.1.call-start = ((), (), s32[]{:S(2)}) async-start(), calls=%async_computation.1 | async-start | bytes 7864320 | tf_op jit(solution)/shard_map/all_gather | solution.py:37
  7.9 288.4 %all-gather.6.cloned.1.call-start = ((), (), s32[]{:S(2)}) async-start(), calls=%async_computation.2 | async-start | bytes 37748736 | tf_op jit(solution)/shard_map/all_gather | solution.py:43
  8.6 570.4 %reduce-scatter.4.cloned.1.call-start = ((), (), s32[]{:S(2)}) async-start(), calls=%async_computation.3 | async-start | bytes 8847360 | tf_op jit(solution)/shard_map/reduce_scatter | solution.py:90
  349.5 30.0 %copy-start = (s32[12]{0:T(128)S(1)}, s32[12]{0:T(128)}, u32[]{:S(2)}) copy-start(s32[12]{0:T(128)} %param.10) | copy-start | bytes 148
  398.5 7.1 %collective-permute-start = (bf16[16,4096]{1,0:T(8,128)(2,1)S(1)}, bf16[16,4096]{1,0:T(8,128)(2,1)S(1)}, u32[]{:S(2)}, u32[]{:S(2)}) collective-permute-start(bf16[16,4096]{1,0:T(8,128)(2,1)S(1)} %fusion), channel_id=1, source_target_pairs={{0,1},{1,2},{2,3},{3,4},{4,5},{5,6},{6,7},{8,9},{9,10},{10,11},{11... | collective-permute-start | bytes 393224
  400.1 5.5 collective-permute-start.1
Sparse Core Ops, SparseCore 0:
  9.5 123.9 all-gather.3
  135.4 160.8 all-gather.5
  454.2 124.8 reduce-scatter.3
where the time goes:
time: 590 us
  waiting for transfers between devices  381 us (65%)
  matrix products  74.3 us (13%)
  blocking collectives  70.2 us (12%)
  other arithmetic  38.4 us (7%)
  between operations  14.5 us (2%)
  local copies, waits for them, and re-layouts  6.81 us (1%)
    all_gather x1, waiting for transfers between devices, shards(): whole_head = lax.all_gather(head_weight, 'rows', axis=0, tiled=True)  163 us
    reduce_scatter x1, waiting for transfers between devices, shards(): lax.psum_scatter(partial_terms.astype(jnp.bfloat16), 'vocab', scatter_dim...  125 us
    all_gather x1, waiting for transfers between devices, shards(): lax.all_gather(hidden_pass, 'vocab', axis=2, tiled=True)  91.9 us
    dot_general x1, matrix products, shards(): logits = jnp.dot(tokens, whole_head, preferred_element_type=jnp.float32)  36.8 us
    dot_general x1, matrix products, shards(): lax.dot_general(slopes, whole_head, (((1,), (1,)), ((), ())), preferred_e...  36.4 us
    all_gather x1, blocking collectives, shards(): lax.all_gather(hidden_query, 'vocab', axis=2, tiled=True)  29.5 us
    unnamed x1, blocking collectives  18 us
    mul x1, other arithmetic, pool_rows(): totals = jnp.sum(values ** 4 * weight, axis=1)  14 us
  transfers between devices with their start and end apart: 5, of which 4 were waited for; matrix products, arithmetic and copies ran while one was open for 1% of the time, Pallas kernels for 0%

commit v1 on v0

--- a/solution.py
+++ b/solution.py
@@ -6,6 +6,28 @@
 V = 16384
 MARGIN = 1.0
 SHARPNESS = 16.0
+
+
+def joined_along(blocks, dim):
+    blocks = jnp.moveaxis(blocks, 0, dim)
+    shape = blocks.shape
+    return blocks.reshape(*shape[:dim], shape[dim] * shape[dim + 1], *shape[dim + 2 :])
+
+
+def doubled(array, axis):
+    count = lax.axis_size(axis)
+    parts = array[None]
+    for level in range(count.bit_length() - 1):
+        bit = 1 << level
+        theirs = lax.ppermute(parts, axis, [(i, i ^ bit) for i in range(count)])
+        both = jnp.stack([parts, theirs])
+        upper = lax.axis_index(axis) >> level & 1
+        parts = jnp.where(upper == 0, both, both[::-1]).reshape(-1, *array.shape)
+    return parts
+
+
+def gather_by_bits(x, axis, dim):
+    return joined_along(doubled(x, axis), dim)
 
 
 def activate(logits):
@@ -34,7 +56,7 @@
     query_length = hidden_query.shape[1]
     pass_rows = groups * pass_length
     whole_pass, whole_query = (
-        lax.all_gather(hidden_pass, "vocab", axis=2, tiled=True),
+        gather_by_bits(hidden_pass, "vocab", 2),
         lax.all_gather(hidden_query, "vocab", axis=2, tiled=True),
     )
     tokens = jnp.concatenate(

time: 590 us -> 540 us (0.915); the launches traced: 590 us -> 530 us
  waiting for transfers between devices: 381 us -> 173 us
  blocking collectives: 70.2 us -> 189 us
  local copies, waits for them, and re-layouts: 6.81 us -> 23.2 us
  other arithmetic: 38.4 us -> 46.1 us
    all_gather x1, waiting for transfers between devices: 163 us -> 11.5 us  [shards(): whole_head = lax.all_gather(head_weight, 'rows', axis=0, tiled=True)]
    all_gather x1, blocking collectives: 29.5 us -> 150 us  [shards(): lax.all_gather(hidden_query, 'vocab', axis=2, tiled=True)]
    all_gather x1 -> x0, waiting for transfers between devices: 91.9 us -> none  [shards(): lax.all_gather(hidden_pass, 'vocab', axis=2, tiled=True)]
    ppermute x0 -> x2, waiting for transfers between devices: none -> 34.6 us  [doubled(): theirs = lax.ppermute(parts, axis, [(i, i ^ bit) for i in range(count)])]
    unnamed x6 -> x17, local copies, waits for them, and re-layouts: 2.29 us -> 11.2 us
    reshape x0 -> x1, local copies, waits for them, and re-layouts: none -> 7.49 us  [doubled(): parts = jnp.where(upper == 0, both, both[::-1]).reshape(-1, *array.shape)]
    another operation x0 -> x3, other arithmetic: none -> 7.02 us  [doubled(): both = jnp.stack([parts, theirs])]
  transfers between devices with their start and end apart: 5 -> 6, of which waited for: 4 -> 4; matrix products, arithmetic and copies ran while one was open for 1% -> 6% of each run, Pallas kernels for 0% -> 0%
where the time goes in v1:
time: 540 us; the launch traced here: 530 us
  blocking collectives  189 us (35%)
  waiting for transfers between devices  173 us (32%)
  matrix products  74.3 us (14%)
  other arithmetic  46.1 us (9%)
  local copies, waits for them, and re-layouts  23.2 us (4%)
  between operations  15.3 us (3%)
  starting transfers between devices  8.66 us (2%)
    all_gather x1, blocking collectives, shards(): lax.all_gather(hidden_query, 'vocab', axis=2, tiled=True)  150 us
    reduce_scatter x1, waiting for transfers between devices, shards(): lax.psum_scatter(partial_terms.astype(jnp.bfloat16), 'vocab', scatter_dim...  126 us
    dot_general x1, matrix products, shards(): logits = jnp.dot(tokens, whole_head, preferred_element_type=jnp.float32)  36.8 us
    dot_general x1, matrix products, shards(): lax.dot_general(slopes, whole_head, (((1,), (1,)), ((), ())), preferred_e...  36.4 us
    ppermute x2, waiting for transfers between devices, doubled(): theirs = lax.ppermute(parts, axis, [(i, i ^ bit) for i in range(count)])  34.6 us
    unnamed x1, blocking collectives  19.4 us
    mul x1, other arithmetic, pool_rows(): totals = jnp.sum(values ** 4 * weight, axis=1)  14 us
    convert_element_type x2, other arithmetic, logit_slopes(): return gradient.astype(jnp.bfloat16).reshape(groups * length, -1)  13.3 us
  transfers between devices with their start and end apart: 6, of which 4 were waited for; matrix products, arithmetic and copies ran while one was open for 6% of the time, Pallas kernels for 0%

profile of v1, /device:TPU:0, one launch (start us, length us, event | category | flops | bytes accessed | tf_op | source)
XLA Modules:
  0.0 529.8 jit_solution(3018798428975567268)
XLA Ops:
  7.2 0.7 all-gather.3.cloned.1.call-update
  7.9 3.1 collective-permute-start
  11.1 34.6 %collective-permute-done = bf16[1,12,64,1024]{3,2,1,0:T(8,128)(2,1)S(1)} collective-permute-done((bf16[1,12,64,1024]{3,2,1,0:T(8,128)(2,1)}, bf16[1,12,64,1024]{3,2,1,0:T(8,128)(2,1)S(1)}, u32[]{:S(2)}, u32[]{:S(2)}) %collective-permute-start) | collective-permute-done | bytes 1572896 | tf_op jit(solution)/shard_map/ppermute | solution.py:22
  45.7 1.7 pad_maximum_fusion.1
  47.4 2.9 fusion.16
  50.3 2.8 collective-permute-start.1
  53.3 0.6 dynamic-slice.4
  54.5 149.9 %all_gather.9 = bf16[12,8,4096]{2,1,0:T(8,128)(2,1)} all-gather(bf16[12,8,1024]{2,1,0:T(8,128)(2,1)S(1)} %copy-done.1), channel_id=1, replica_groups=mesh['vocab'=4,'rows'=8] {'vocab'}, dimensions={2}, use_global_device_ids=true | all-gather | bytes 983040 | tf_op jit(solution)/shard_map/all_gather | solution.py:60
  204.5 2.5 pad_maximum_fusion
  207.0 2.1 reverse_select_fusion
  209.1 7.5 %copy.13 = bf16[4,12,64,1024]{3,0,2,1:T(4,128)(2,1)} copy(bf16[4,12,64,1024]{3,2,1,0:T(8,128)(2,1)S(1)} %bitcast.42) | data formatting | bytes 12582912 | tf_op jit(solution)/shard_map/reshape | solution.py:25
  216.6 9.5 %copy.16 = bf16[96,8,4,1024]{3,1,2,0:T(8,128)(2,1)} copy(bf16[96,8,4,1024]{3,2,1,0:T(4,128)(2,1)} %bitcast.43) | data formatting | bytes 12582912
  226.1 11.5 %all-gather.3.cloned.1.call-done = bf16[4096,4096]{1,0:T(8,128)(2,1)} async-done(((bf16[512,4096]{1,0:T(8,128)(2,1)}), bf16[4096,4096]{1,0:T(8,128)(2,1)}) %all-gather.3.cloned.1.call-update) | async-done | bytes 33554448 | tf_op jit(solution)/shard_map/all_gather | solution.py:65
  237.7 36.8 %fusion.4 = f32[864,4096]{1,0:T(8,128)} fusion(bf16[4096,4096]{1,0:T(8,128)(2,1)} %all-gather.3.cloned.1.call-done, bf16[96,4096]{1,0:T(8,128)(2,1)S(1)} %bitcast.49, bf16[768,4096]{1,0:T(8,128)(2,1)} %bitcast.44), kind=kOutput, calls=%fused_computation.9 | convolution fusion | flops 29005185024 | bytes 54788096 | tf_op jit(solution)/shard_map/dot_general | solution.py:66
  274.4 14.0 %multiply_multiply_fusion.1 = f32[768,4096]{1,0:T(8,128)} fusion(f32[864,4096]{1,0:T(8,128)} %fusion.4), kind=kLoop, calls=%fused_computation.1 | loop fusion | flops 9437184 | bytes 25165824 | tf_op jit(solution)/shard_map/mul | solution.py:40
  288.4 2.4 fusion.19
  290.9 6.6 %multiply_reduce_fusion = f32[12,4096]{1,0:T(8,128)S(1)} fusion(f32[12,64,4096]{2,1,0:T(8,128)} %bitcast.41, f32[12,64]{1,0:T(8,128)S(1)} %convert_element_type.48), kind=kLoop, calls=%fused_computation.7 | loop fusion | flops 6242304 | bytes 12782592 | tf_op jit(solution)/shard_map/reduce_sum | solution.py:40
  297.6 10.9 %all-gather = bf16[8,12,4096]{2,1,0:T(8,128)(2,1)S(1)} all-gather(bf16[1,12,4096]{2,1,0:T(8,128)(2,1)S(1)} %fusion.23), channel_id=1, replica_groups=mesh['vocab'=4,'rows'=8] {'rows'}, dimensions={0}, use_global_device_ids=true | all-gather | bytes 884736 | tf_op jit(solution)/shard_map/all_gather | solution.py:73
  308.7 0.3 fusion.24
  309.0 8.8 %psum.7 = f32[12,96]{1,0:T(8,128)S(1)} all-reduce(f32[12,96]{1,0:T(8,128)S(1)} %fusion.24), channel_id=1, replica_groups=mesh['vocab'=4,'rows'=8] {'vocab'}, use_global_device_ids=true, to_apply=%region_2.3 | all-reduce | flops 1152 | bytes 9216 | tf_op jit(solution)/shard_map/psum | solution.py:78
  318.2 0.5 convolution_convert_fusion
  318.7 19.4 %fusion = bf16[16,4096]{1,0:T(8,128)(2,1)S(1)} fusion(bf16[96,4096]{1,0:T(8,128)(2,1)S(1)} %convolution_convert_fusion), kind=kCustom, calls=%all-reduce-scatter | all-reduce-scatter fusion | flops 524289 | bytes 918016
  338.2 1.3 collective-permute-start.2
  339.5 0.3 convolution_multiply_fusion
  339.8 1.4 collective-permute-start.3
  341.2 2.3 fusion.22
  343.7 0.8 concatenate.8
  344.7 11.0 %fusion.3 = bf16[768,4096]{1,0:T(8,128)(2,1)} fusion(f32[864,4096]{1,0:T(8,128)} %fusion.4, f32[768]{0:T(1024)S(1)} %mul.135, f32[12,4096]{1,0:T(8,128)S(1)} %power_multiply_fusion), kind=kLoop, calls=%fused_computation.4 | loop fusion | flops 28311552 | bytes 19074048 | tf_op jit(solution)/shard_map/convert_element_type | solution.py:50
  355.7 36.4 %fusion.12 = bf16[864,4096]{1,0:T(8,128)(2,1)} fusion(bf16[4096,4096]{1,0:T(8,128)(2,1)} %all-gather.3.cloned.1.call-done, bf16[96,4096]{1,0:T(8,128)(2,1)S(1)} %fusion.22, bf16[768,4096]{1,0:T(8,128)(2,1)} %fusion.3), kind=kOutput, calls=%fused_computation.17 | convolution fusion | flops 29008723968 | bytes 47710208 | tf_op jit(solution)/shard_map/dot_general | solution.py:109
  392.1 126.2 %reduce-scatter.4.cloned.1.call-done = bf16[864,1024]{1,0:T(8,128)(2,1)} async-done(((bf16[864,4096]{1,0:T(8,128)(2,1)}), bf16[864,1024]{1,0:T(8,128)(2,1)}) %reduce-scatter.4.cloned.1.call-update) | async-done | bytes 1769488 | tf_op jit(solution)/shard_map/reduce_scatter | solution.py:112
  518.3 2.7 slice.20
  521.0 1.6 slice_bitcast_fusion
  (29 shorter events, 1.5 us)
Async XLA Ops:
  7.2 230.5 %all-gather.3.cloned.1.call-start = ((), (), s32[]{:S(2)}) async-start(), calls=%async_computation.1 | async-start | bytes 37748736 | tf_op jit(solution)/shard_map/all_gather | solution.py:65
  7.9 510.4 %reduce-scatter.4.cloned.1.call-start = ((), (), s32[]{:S(2)}) async-start(), calls=%async_computation.2 | async-start | bytes 8847360 | tf_op jit(solution)/shard_map/reduce_scatter | solution.py:112
  7.9 37.7 %collective-permute-start = (bf16[1,12,64,1024]{3,2,1,0:T(8,128)(2,1)}, bf16[1,12,64,1024]{3,2,1,0:T(8,128)(2,1)S(1)}, u32[]{:S(2)}, u32[]{:S(2)}) collective-permute-start(bf16[1,12,64,1024]{3,2,1,0:T(8,128)(2,1)} %bitcast.46), channel_id=1, source_target_pairs={{0,8},{8,0},{16,24},{24,16},{1,9},{9,1},{17,25},{25,17},{2,10},{10... | collective-permute-start | bytes 4718600 | tf_op jit(solution)/shard_map/ppermute | solution.py:22
  47.4 5.7 %copy-start.3 = (s32[12,64]{1,0:T(8,128)S(1)}, s32[12,64]{1,0:T(8,128)}, u32[]{:S(2)}) copy-start(s32[12,64]{1,0:T(8,128)} %param.8) | copy-start | bytes 9220
  47.4 5.7 %copy-start.4 = (s32[12,8]{0,1:T(8,128)S(1)}, s32[12,8]{0,1:T(8,128)}, u32[]{:S(2)}) copy-start(s32[12,8]{0,1:T(8,128)} %param.9) | copy-start | bytes 1156
  47.4 5.9 %copy-start.5 = (u32[32]{0:T(128)S(1)}, u32[32]{0:T(128)}, u32[]{:S(2)}) copy-start(u32[32]{0:T(128)} %constant.38) | copy-start | bytes 388
  47.4 7.1 %copy-start.1 = (bf16[12,8,1024]{2,1,0:T(8,128)(2,1)S(1)}, bf16[12,8,1024]{2,1,0:T(8,128)(2,1)}, u32[]{:S(2)}) copy-start(bf16[12,8,1024]{2,1,0:T(8,128)(2,1)} %param.7) | copy-start | bytes 589828
  50.3 154.2 %collective-permute-start.1 = (bf16[2,12,64,1024]{3,2,1,0:T(8,128)(2,1)}, bf16[2,12,64,1024]{3,2,1,0:T(8,128)(2,1)}, u32[]{:S(2)}, u32[]{:S(2)}) collective-permute-start(bf16[2,12,64,1024]{3,2,1,0:T(8,128)(2,1)} %get-tuple-element.3), channel_id=1, source_target_pairs={{0,16},{8,24},{16,0},{24,8},{1,17},{9,25},{17,1},{25,9},{2,18},{10... | collective-permute-start | bytes 9437192 | tf_op jit(solution)/shard_map/ppermute | solution.py:22
  216.6 21.1 %copy-start = (bf16[12,8,4096]{2,1,0:T(8,128)(2,1)S(1)}, bf16[12,8,4096]{2,1,0:T(8,128)(2,1)}, u32[]{:S(2)}) copy-start(bf16[12,8,4096]{2,1,0:T(8,128)(2,1)} %all_gather.9) | copy-start | bytes 2359300
  290.9 26.9 %copy-start.2 = (s32[12]{0:T(128)S(1)}, s32[12]{0:T(128)}, u32[]{:S(2)}) copy-start(s32[12]{0:T(128)} %param.10) | copy-start | bytes 148
  338.2 5.5 %collective-permute-start.2 = (bf16[16,4096]{1,0:T(8,128)(2,1)S(1)}, bf16[16,4096]{1,0:T(8,128)(2,1)S(1)}, u32[]{:S(2)}, u32[]{:S(2)}) collective-permute-start(bf16[16,4096]{1,0:T(8,128)(2,1)S(1)} %fusion), channel_id=1, source_target_pairs={{0,1},{1,2},{2,3},{3,4},{4,5},{5,6},{6,7},{8,9},{9,10},{10,11},{11... | collective-permute-start | bytes 393224
  339.8 3.9 collective-permute-start.3
Sparse Core Ops, SparseCore 0:
  9.9 163.3 all-gather.2
  392.2 126.0 reduce-scatter.3
